TPU v7x, 256 devices: a whole 4x4x8 slice. The times are simulated.
256 devices in a mesh: win: 4 (over y_lo, core), tile: 64 (over x, y_hi, z).
Axes of the slice: x: 4, y: 4 (y_hi: 2, y_lo: 2; y = y_hi * 2 + y_lo), z: 8, core: 2. Of those that a mesh axis runs over, the one named last changes fastest.
Arguments:
- initial: float32 [4, 64, 36, 4096], P('win', 'tile'), may hold values from -6 to 6
- courant_x: bfloat16 [4, 64, 36, 4096], P('win', 'tile'), may hold values from 0.099609375 to 2.890625
- courant_y: bfloat16 [4, 64, 36, 4096], P('win', 'tile'), may hold values from 0.099609375 to 2.890625
- observed: float32 [4, 64, 64, 64], P('win', 'tile'), may hold values from -3 to 3
- precision_w: float32 [4, 64, 64, 64], P('win', 'tile'), may hold values from 0.2 to 2
- kernel: float32 [36], replicated, may hold values from 0.1 to 1
- profile: float32 [36], replicated, may hold values from 0.05 to 1
- emission: float32 [64, 64, 64], P('tile'), may hold values from -6 to 6
- edges: int32 [6, 64], replicated, may hold values from 0 to 63, as said below
Outputs:
- gradient: float32 [64, 64, 64], P('tile', 'win')
Inputs may be any that keep to these rules, and one draw needn't show every extreme that they name: edges[0, t] is (t - 1) or (t - 16) modulo 64, and edges[3, t] is (t - 2) or (t - 32) modulo 64; each of the four occurs for some tile; rows 1, 2, 4 and 5 hold 0 or 1, each value at some tile.
All inputs are finite; a program needn't handle non-finite values.
Results may differ from a plain program's by a relative error of at most 0.0003.
Values sent between devices are 32-bit elements; how exact they have to be, the bound alone decides.
A program may use at most 64 MiB of HBM per device.

v0:
```python
import jax
import jax.numpy as jnp
from jax import lax
from jax.sharding import PartitionSpec as P

STEPS = 2


def from_behind(block, axis, distance):
    devices = range(lax.axis_size(axis))
    route = [((i - distance) % len(devices), i) for i in devices]
    return lax.ppermute(block, axis, route)


def advect_along(tracer_field, rim_cells, courant, along):
    side_len = tracer_field.shape[along]
    extended = jnp.concatenate([rim_cells, tracer_field], along)
    edge_speed = lax.slice_in_dim(courant, side_len - 1, side_len, axis=along)
    inflow = jnp.zeros_like(tracer_field)
    outlet = jnp.zeros_like(edge_speed)
    for depth in range(1, 4):
        inflow = inflow + lax.slice_in_dim(
            extended, 3 - depth, 3 - depth + side_len, axis=along
        ) * jnp.clip(courant - (depth - 1), 0.0, 1.0)
        outlet = outlet + lax.slice_in_dim(
            tracer_field, side_len - depth, side_len - depth + 1, axis=along
        ) * jnp.clip(edge_speed - (depth - 1), 0.0, 1.0)
    outflow = jnp.concatenate([lax.slice_in_dim(inflow, 1, side_len, axis=along), outlet], along)
    return tracer_field - (outflow - inflow)


def advect_adjoint(sensitivity, courant, along):
    rim_shape = list(sensitivity.shape)
    rim_shape[along] = 3
    blank_field = jnp.zeros_like(sensitivity)
    blank_rim = jnp.zeros(tuple(rim_shape), jnp.float32)
    unused, pullback = jax.vjp(
        lambda tracer_field, rim_cells: advect_along(tracer_field, rim_cells, courant, along),
        blank_field,
        blank_rim,
    )
    return pullback(sensitivity)


def strips(tracer_field):
    side_len = tracer_field.shape[-1]
    east_strip = jnp.swapaxes(tracer_field[..., side_len - 3 :][..., ::-1], -1, -2)
    north_strip = tracer_field[..., side_len - 3 :, :][..., ::-1, :]
    return (east_strip, north_strip)


def add_strips(tracer_field_adjoint, east_bar, north_bar):
    side_len = tracer_field_adjoint.shape[-1]
    tracer_field_adjoint = tracer_field_adjoint.at[..., side_len - 3 :].add(
        jnp.swapaxes(east_bar, -1, -2)[..., ::-1]
    )
    return tracer_field_adjoint.at[..., side_len - 3 :, :].add(north_bar[..., ::-1, :])


def as_halo(panel, along):
    if along == 3:
        return jnp.swapaxes(panel[..., ::-1, :], -1, -2)
    return panel[..., ::-1, :]


def halo_back(rim_bar, along):
    if along == 3:
        return jnp.swapaxes(rim_bar, -1, -2)[..., ::-1, :]
    return rim_bar[..., ::-1, :]


def reverse_along(panel, flagged):
    return jnp.where(flagged, panel[..., ::-1], panel)


def own_entries(edges, position, base, tile_count, nearest):
    entries = lax.dynamic_slice_in_dim(edges, position, 1, 1)[:, 0]
    distant_indicator = entries[base] != (position - nearest) % tile_count
    return (distant_indicator, entries[base + 1], entries[base + 2])


def collect_receiver_index(tracer_field, local_details, shift_amounts, transfer_buffer):
    east_strip, north_strip = strips(tracer_field)
    stacked_panels = jnp.stack([east_strip, north_strip])
    received_neighbor = transfer_buffer(stacked_panels, shift_amounts[0])
    received_distant = transfer_buffer(stacked_panels, shift_amounts[1])
    distant_indicator, edge_code, flip_code = local_details
    arrived = jnp.where(distant_indicator, received_distant, received_neighbor)
    panel = jnp.where(edge_code == 0, arrived[0], arrived[1])
    return reverse_along(panel, flip_code == 1)


def backward_receiver_index(
    tracer_field_adjoint, panel_adjoint_value, local_details, shift_amounts, transfer_buffer
):
    distant_indicator, edge_code, flip_code = local_details
    returned = reverse_along(panel_adjoint_value, flip_code == 1)
    blank_panel = jnp.zeros_like(returned)
    stacked_panels = jnp.stack(
        [
            jnp.where(edge_code == 0, returned, blank_panel),
            jnp.where(edge_code == 0, blank_panel, returned),
        ]
    )
    empty_stacked_panels = jnp.zeros_like(stacked_panels)
    received_neighbor = transfer_buffer(
        jnp.where(distant_indicator, empty_stacked_panels, stacked_panels), -shift_amounts[0]
    )
    received_distant = transfer_buffer(
        jnp.where(distant_indicator, stacked_panels, empty_stacked_panels), -shift_amounts[1]
    )
    summed = received_neighbor + received_distant
    return add_strips(tracer_field_adjoint, summed[0], summed[1])


def body(initial, courant_x, courant_y, observed, precision_w, kernel, profile, emission, edges):
    side_len = observed.shape[-1]
    cube_shape = (initial.shape[0], initial.shape[2], side_len, side_len)
    tracer = initial[:, 0].reshape(cube_shape)
    speed_x = courant_x[:, 0].astype(jnp.float32).reshape(cube_shape)
    speed_y = courant_y[:, 0].astype(jnp.float32).reshape(cube_shape)
    source_rate = profile[None, :, None, None] * emission[0][None, None]
    tile_count = lax.axis_size("tile")
    position = lax.axis_index("tile")
    offsets_x = (1, tile_count // 4)
    offsets_y = (2, tile_count // 2)
    own_x = own_entries(edges, position, 0, tile_count, 1)
    own_y = own_entries(edges, position, 3, tile_count, 2)

    def carry_x(payload, offset):
        return from_behind(payload, "tile", offset)

    def carry_y(payload, offset):
        return from_behind(payload, "tile", offset)

    def return_x(payload, offset):
        return from_behind(payload, "tile", offset)

    def return_y(payload, offset):
        return from_behind(payload, "tile", offset)

    for step_index in range(STEPS):
        tracer = advect_along(
            tracer,
            as_halo(collect_receiver_index(tracer, own_x, offsets_x, carry_x), 3),
            speed_x,
            3,
        )
        tracer = advect_along(
            tracer,
            as_halo(collect_receiver_index(tracer, own_y, offsets_y, carry_y), 2),
            speed_y,
            2,
        )
        tracer = tracer + source_rate
    weight_sum = jnp.sum(kernel)
    column = jnp.sum(kernel[None, :, None, None] * tracer, axis=1) / weight_sum
    misfit = column - observed[:, 0]
    adjoint = (precision_w[:, 0] * misfit)[:, None] * (kernel[None, :, None, None] / weight_sum)
    gradient = jnp.zeros(emission.shape[1:], jnp.float32)
    for step_index in range(STEPS):
        gradient = gradient + jnp.sum(profile[None, :, None, None] * adjoint, axis=(0, 1))
        if step_index + 1 < STEPS:
            adjoint, rim_bar = advect_adjoint(adjoint, speed_y, 2)
            adjoint = backward_receiver_index(
                adjoint, halo_back(rim_bar, 2), own_y, offsets_y, return_y
            )
            adjoint, rim_bar = advect_adjoint(adjoint, speed_x, 3)
            adjoint = backward_receiver_index(
                adjoint, halo_back(rim_bar, 3), own_x, offsets_x, return_x
            )
    summed_all = lax.psum(gradient, "win")
    row_count = gradient.shape[0] // lax.axis_size("win")
    share_rows = lax.dynamic_slice_in_dim(
        summed_all, lax.axis_index("win") * row_count, row_count, 0
    )
    return share_rows[None]


def solution(mesh):
    placed = (
        P("win", "tile", None, None),
        P("win", "tile", None, None),
        P("win", "tile", None, None),
        P("win", "tile", None, None),
        P("win", "tile", None, None),
        P(),
        P(),
        P("tile", None, None),
        P(),
    )
    return jax.shard_map(
        body, mesh=mesh, in_specs=placed, out_specs=P("tile", "win", None), check_vma=False
    )
```

profile of v0, /device:TPU:1, one launch (start us, length us, event | category | flops | bytes accessed | tf_op | source)
XLA Modules:
  0.0 277.5 jit_solution(16219852052872074876)
XLA Ops:
  27.1 3.3 %rev.75 = f32[1,36,3,64]{2,1,3,0:T(8,128)} reverse(f32[1,36,3,64]{2,1,3,0:T(8,128)} %reverse_select_fusion.1), dimensions={2} | reverse | bytes 55296 | tf_op jit(solution)/shard_map/rev | solution.py:62
  30.5 5.5 %fusion.53 = (f32[1,36,64,64]{3,1,2,0:T(8,128)S(1)}, f32[1,36,64,64]{3,1,2,0:T(8,128)}) fusion(f32[1,36,64,64]{3,2,0,1:T(8,128)} %reshape.545, f32[1,36,64,64]{3,1,2,0:T(8,128)S(1)} %copy.200, f32[1,36,64,3]{3,1,2,0:T(8,128)} %bitcast.80), kind=kLoop, calls=%fused_computation.160 | loop fusion | flops 1916928 | bytes 2386944 | tf_op jit(solution)/shard_map/convert_element_type | solution.py:120
  40.8 2.8 %fusion.24 = f32[1,36,64,1]{3,1,2,0:T(8,128)S(1)} fusion(f32[1,36,64,1]{3,1,2,0:T(8,128)} %copy.199, f32[1,36,64,64]{3,1,2,0:T(8,128)S(1)} %copy.200, f32[1,36,64,64]{3,1,2,0:T(8,128)S(1)} %get-tuple-element.82), kind=kLoop, calls=%fused_computation.53 | loop fusion | flops 18432 | bytes 55296 | tf_op jit(solution)/shard_map/add | solution.py:25
  56.4 7.5 %collective-permute-done.3 = f32[2,1,36,3,64]{4,2,3,1,0:T(8,128)S(1)} collective-permute-done((f32[2,1,36,3,64]{4,2,3,1,0:T(8,128)S(1)}, f32[2,1,36,3,64]{4,2,3,1,0:T(8,128)S(1)}, u32[]{:S(2)}, u32[]{:S(2)}) %collective-permute-start.3) | collective-permute-done | bytes 55328 | tf_op jit(solution)/shard_map/ppermute | solution.py:12
  72.0 3.8 %fusion.17 = f32[1,36,64,1]{3,1,2,0:T(8,128)} fusion(f32[1,36,64,1]{3,1,2,0:T(8,128)} %copy.199, f32[1,36,64,64]{3,1,2,0:T(8,128)S(1)} %multiply_add_fusion.1, f32[1,36,64,64]{3,1,2,0:T(8,128)S(1)} %get-tuple-element.82), kind=kLoop, calls=%fused_computation.38 | loop fusion | flops 18432 | bytes 55296 | tf_op jit(solution)/shard_map/add | solution.py:25
  87.2 3.3 %rev.83 = f32[1,36,3,64]{2,1,3,0:T(8,128)} reverse(f32[1,36,3,64]{2,1,3,0:T(8,128)} %reverse_select_fusion), dimensions={2} | reverse | bytes 55296 | tf_op jit(solution)/shard_map/rev | solution.py:62
  90.5 4.4 %fusion.20 = f32[1,36,64,64]{3,1,2,0:T(8,128)S(1)} fusion(f32[1,36,64,64]{3,1,2,0:T(8,128)S(1)} %multiply_add_fusion.1, f32[1,36,64,3]{3,1,2,0:T(8,128)} %bitcast.79, f32[1,36,64,64]{3,2,0,1:T(8,128)} %reshape.545), kind=kLoop, calls=%fused_computation.44 | loop fusion | flops 1916928 | bytes 1797120 | tf_op jit(solution)/shard_map/add | solution.py:22
  101.5 4.0 %collective-permute-done.6 = f32[2,1,36,3,64]{4,2,3,1,0:T(8,128)S(1)} collective-permute-done((f32[2,1,36,3,64]{4,2,3,1,0:T(8,128)S(1)}, f32[2,1,36,3,64]{4,2,3,1,0:T(8,128)S(1)}, u32[]{:S(2)}, u32[]{:S(2)}) %collective-permute-start.6) | collective-permute-done | bytes 55328 | tf_op jit(solution)/shard_map/ppermute | solution.py:12
  105.5 5.7 %collective-permute-done.7 = f32[2,1,36,3,64]{4,2,3,1,0:T(8,128)S(1)} collective-permute-done((f32[2,1,36,3,64]{4,2,3,1,0:T(8,128)S(1)}, f32[2,1,36,3,64]{4,2,3,1,0:T(8,128)S(1)}, u32[]{:S(2)}, u32[]{:S(2)}) %collective-permute-start.7) | collective-permute-done | bytes 55328 | tf_op jit(solution)/shard_map/ppermute | solution.py:12
  111.4 3.3 %fusion.5 = (f32[1,36,64,64]{3,1,2,0:T(8,128)S(1)}, f32[1,36,64,64]{3,1,2,0:T(8,128)}) fusion(f32[1,36,64,64]{3,1,2,0:T(8,128)S(1)} %copy-done.5, f32[1,36,3,64]{3,1,2,0:T(8,128)S(1)} %rev.87, f32[1,36,64,64]{3,2,0,1:T(8,128)} %reshape.546), kind=kLoop, calls=%fused_computation.20 | loop fusion | flops 1916928 | bytes 2386944 | tf_op jit(solution)/shard_map/add | solution.py:22
  121.5 2.9 %copy.219 = f32[1,36,64,64]{2,1,3,0:T(8,128)} copy(f32[1,36,64,64]{3,1,2,0:T(8,128)} %get-tuple-element.79) | data formatting | bytes 1179648 | tf_op jit(solution)/shard_map/jit(clip)/min | solution.py:24
  126.0 3.6 %fusion.51 = (f32[1,36,64,64]{2,1,3,0:T(8,128)}, f32[1,36,64,64]{2,1,3,0:T(8,128)}) fusion(f32[1,36,64,64]{2,1,3,0:T(8,128)} %copy.219, f32[1,36,63,64]{2,1,3,0:T(8,128)} %copy.271, f32[36]{0:T(128)S(1)} %broadcast_divide_fusion, f32[64,64]{0,1:T(8,128)S(1)} %copy.212), kind=kLoop, calls=%fused_computation.158 | loop fusion | flops 442368 | bytes 2366608 | tf_op jit(solution)/shard_map/transpose(jvp())/mul | solution.py:22
  129.6 2.9 %copy.217 = f32[1,36,64,64]{3,1,2,0:T(8,128)} copy(f32[1,36,64,64]{2,1,3,0:T(8,128)} %get-tuple-element.56) | data formatting | bytes 1179648 | tf_op jit(solution)/shard_map/transpose(jvp())/add_any | solution.py:28
  140.1 2.6 rev.88
  142.7 2.6 rev.89
  145.3 2.9 %copy.250 = f32[1,36,64,64]{3,1,2,0:T(8,128)} copy(f32[1,36,64,64]{2,1,3,0:T(8,128)} %split.34) | data formatting | bytes 1179648
  149.7 2.7 pad_maximum_fusion
  156.9 2.6 copy.225
  166.7 17.9 %scatter-add.14 = f32[1,36,64,64]{3,1,2,0:T(8,128)S(1)} dynamic-update-slice(f32[1,36,64,64]{3,1,2,0:T(8,128)S(1)} %add_add_fusion, f32[1,36,64,3]{3,1,2,0:T(8,128)} %copy.231, s32[]{:T(128)} %constant.141.clone.1, s32[]{:T(128)} %constant.141.clone.1, s32[]{:T(128)} %constant.141.clone.1, s32[]{:T(128)} %constant.153.clone.1) | dynamic-update-slice | bytes 55300 | tf_op jit(solution)/shard_map/scatter-add | solution.py:54
  187.5 4.1 %fusion.40 = (f32[1,36,64,1]{3,1,2,0:T(8,128)}, f32[1,36,64,1]{3,1,2,0:T(8,128)}, f32[1,36,64,1]{3,1,2,0:T(8,128)}) fusion(f32[1,36,64,64]{3,1,2,0:T(8,128)S(1)} %get-tuple-element.82, f32[1,36,64,64]{3,1,2,0:T(8,128)} %neg.17), kind=kLoop, calls=%fused_computation.103 | loop fusion | flops 11520 | bytes 46080 | tf_op jit(solution)/shard_map/transpose(jvp())/mul | solution.py:25
  195.0 2.6 rev.92
  197.6 2.6 rev.93
  206.2 2.7 fusion
  211.4 3.5 %collective-permute-start.10 = (f32[2,1,36,3,64]{4,0,3,2,1:T(2,128)S(1)}, f32[2,1,36,3,64]{4,0,3,2,1:T(2,128)S(1)}, u32[]{:S(2)}, u32[]{:S(2)}) collective-permute-start(f32[2,1,36,3,64]{4,0,3,2,1:T(2,128)S(1)} %copy.238), channel_id=1, source_target_pairs={{1,0},{2,1},{3,2},{4,3},{5,4},{6,5},{7,6},{8,7},{9,8},{10,9},{11,1... | collective-permute-start | bytes 165896 | tf_op jit(solution)/shard_map/ppermute | solution.py:12
  214.9 2.6 copy.239
  225.5 2.8 %add.201 = f32[2,1,36,3,64]{3,2,4,1,0:T(8,128)S(1)} add(f32[2,1,36,3,64]{3,2,4,1,0:T(8,128)} %copy.240, f32[2,1,36,3,64]{3,2,4,1,0:T(8,128)} %copy.241) | non-fusion elementwise | flops 13824 | bytes 165888 | tf_op jit(solution)/shard_map/add | solution.py:112
  229.6 3.3 %rev.94 = f32[1,36,64,3]{3,1,2,0:T(8,128)} reverse(f32[1,36,64,3]{3,1,2,0:T(8,128)} %get-tuple-element.61), dimensions={3} | reverse | bytes 55296 | tf_op jit(solution)/shard_map/rev | solution.py:55
  232.9 2.9 %add.202 = f32[1,36,64,3]{3,1,2,0:T(8,128)} add(f32[1,36,64,3]{3,1,2,0:T(8,128)} %copy.252, f32[1,36,64,3]{3,1,2,0:T(8,128)} %rev.94) | non-fusion elementwise | flops 6912 | bytes 82944 | tf_op jit(solution)/shard_map/add | solution.py:54
  237.6 2.6 rev.95
  240.2 2.8 %slice_add_fusion = f32[1,36,3,64]{2,1,3,0:T(8,128)} fusion(f32[1,36,3,64]{2,1,3,0:T(8,128)} %rev.95, f32[1,36,64,64]{2,1,3,0:T(8,128)S(1)} %constant_dynamic-update-slice_fusion), kind=kLoop, calls=%fused_computation.32 | loop fusion | flops 6912 | bytes 82944 | tf_op jit(solution)/shard_map/add | solution.py:57
  243.0 18.0 %scatter-add.19 = f32[1,36,64,64]{2,1,3,0:T(8,128)S(1)} dynamic-update-slice(f32[1,36,64,64]{2,1,3,0:T(8,128)S(1)} %constant_dynamic-update-slice_fusion, f32[1,36,3,64]{2,1,3,0:T(8,128)} %slice_add_fusion, s32[]{:T(128)} %constant.141.clone.1, s32[]{:T(128)} %constant.141.clone.1, s32[]{:T(128)} %constant.153.clone.1, s32[]{:T(128)} %constant.141.clone.1) | dynamic-update-slice | bytes 55300 | tf_op jit(solution)/shard_map/scatter-add | solution.py:57
  261.6 15.0 %psum.7 = f32[64,64]{0,1:T(8,128)S(1)} all-reduce(f32[64,64]{0,1:T(8,128)S(1)} %add.204), channel_id=1, replica_groups=mesh['win'=4,'tile'=64] {'win'}, use_global_device_ids=true, to_apply=%region_4.5 | all-reduce | flops 4096 | bytes 32768 | tf_op jit(solution)/shard_map/psum | solution.py:172
  (198 shorter events, 122.9 us)
Async XLA Ops:
  0.0 11.2 %copy-start = (s32[6,64]{1,0:T(8,128)S(1)}, s32[6,64]{1,0:T(8,128)}, u32[]{:S(2)}) copy-start(s32[6,64]{1,0:T(8,128)} %param.25) | copy-start | bytes 4612
  3.0 8.9 %copy-start.6 = (f32[1,36,64,64]{3,2,0,1:T(8,128)}, f32[1,36,64,64]{3,2,0,1:T(8,128)S(1)}, u32[]{:S(2)}) copy-start(f32[1,36,64,64]{3,2,0,1:T(8,128)S(1)} %reshape_squeeze.3) | copy-start | bytes 1769476
  7.3 5.3 %copy-start.22 = (bf16[1,1,36,4096]{3,2,1,0:T(8,128)(2,1)S(1)}, bf16[1,1,36,4096]{3,2,1,0:T(8,128)(2,1)}, u32[]{:S(2)}) copy-start(bf16[1,1,36,4096]{3,2,1,0:T(8,128)(2,1)} %param.18) | copy-start | bytes 884740
  7.3 9.4 %collective-permute-start = (f32[2,1,36,3,64]{4,0,3,2,1:T(2,128)S(1)}, f32[2,1,36,3,64]{4,0,3,2,1:T(2,128)S(1)}, u32[]{:S(2)}, u32[]{:S(2)}) collective-permute-start(f32[2,1,36,3,64]{4,0,3,2,1:T(2,128)S(1)} %pad_maximum_fusion.9), channel_id=1, source_target_pairs={{48,0},{49,1},{50,2},{51,3},{52,4},{53,5},{54,6},{55,7},{56,8},{57... | collective-permute-start | bytes 165896 | tf_op jit(solution)/shard_map/ppermute | solution.py:12
  9.4 12.0 %collective-permute-start.1 = (f32[2,1,36,3,64]{4,0,3,2,1:T(2,128)S(1)}, f32[2,1,36,3,64]{4,0,3,2,1:T(2,128)S(1)}, u32[]{:S(2)}, u32[]{:S(2)}) collective-permute-start(f32[2,1,36,3,64]{4,0,3,2,1:T(2,128)S(1)} %pad_maximum_fusion.9), channel_id=1, source_target_pairs={{63,0},{0,1},{1,2},{2,3},{3,4},{4,5},{5,6},{6,7},{7,8},{8,9},{9,10... | collective-permute-start | bytes 165896 | tf_op jit(solution)/shard_map/ppermute | solution.py:12
  12.6 3.5 %copy-start.28 = (f32[36]{0:T(128)S(1)}, f32[36]{0:T(128)}, u32[]{:S(2)}) copy-start(f32[36]{0:T(128)} %param.22) | copy-start | bytes 436
  40.7 2.8 %copy-start.11 = (f32[1,36,64,64]{3,1,2,0:T(8,128)S(1)}, f32[1,36,64,64]{3,1,2,0:T(8,128)}, u32[]{:S(2)}) copy-start(f32[1,36,64,64]{3,1,2,0:T(8,128)} %get-tuple-element.83) | copy-start | bytes 1769476
  45.8 20.6 %copy-start.2 = (f32[1,36,64,64]{3,1,2,0:T(8,128)}, f32[1,36,64,64]{3,1,2,0:T(8,128)S(1)}, u32[]{:S(2)}) copy-start(f32[1,36,64,64]{3,1,2,0:T(8,128)S(1)} %fusion.30) | copy-start | bytes 1769476
  47.3 5.9 %copy-start.23 = (bf16[1,1,36,4096]{3,2,1,0:T(8,128)(2,1)S(1)}, bf16[1,1,36,4096]{3,2,1,0:T(8,128)(2,1)}, u32[]{:S(2)}) copy-start(bf16[1,1,36,4096]{3,2,1,0:T(8,128)(2,1)} %param.19) | copy-start | bytes 884740
  49.1 7.3 %collective-permute-start.2 = (f32[2,1,36,3,64]{4,2,3,1,0:T(8,128)S(1)}, f32[2,1,36,3,64]{4,2,3,1,0:T(8,128)S(1)}, u32[]{:S(2)}, u32[]{:S(2)}) collective-permute-start(f32[2,1,36,3,64]{4,2,3,1,0:T(8,128)S(1)} %pad_maximum_fusion.6), channel_id=1, source_target_pairs={{32,0},{33,1},{34,2},{35,3},{36,4},{37,5},{38,6},{39,7},{40,8},{41... | collective-permute-start | bytes 165896 | tf_op jit(solution)/shard_map/ppermute | solution.py:12
  50.7 13.2 %collective-permute-start.3 = (f32[2,1,36,3,64]{4,2,3,1,0:T(8,128)S(1)}, f32[2,1,36,3,64]{4,2,3,1,0:T(8,128)S(1)}, u32[]{:S(2)}, u32[]{:S(2)}) collective-permute-start(f32[2,1,36,3,64]{4,2,3,1,0:T(8,128)S(1)} %pad_maximum_fusion.6), channel_id=1, source_target_pairs={{62,0},{63,1},{0,2},{1,3},{2,4},{3,5},{4,6},{5,7},{6,8},{7,9},{8,1... | collective-permute-start | bytes 165896 | tf_op jit(solution)/shard_map/ppermute | solution.py:12
  66.4 1.8 copy-start.3
  66.4 1.8 copy-start.24
  71.8 5.0 %collective-permute-start.4 = (f32[2,1,36,3,64]{4,2,3,1,0:T(8,128)S(1)}, f32[2,1,36,3,64]{4,2,3,1,0:T(8,128)S(1)}, u32[]{:S(2)}, u32[]{:S(2)}) collective-permute-start(f32[2,1,36,3,64]{4,2,3,1,0:T(8,128)S(1)} %pad_maximum_fusion.7), channel_id=1, source_target_pairs={{48,0},{49,1},{50,2},{51,3},{52,4},{53,5},{54,6},{55,7},{56,8},{57... | collective-permute-start | bytes 165896 | tf_op jit(solution)/shard_map/ppermute | solution.py:12
  71.9 9.5 %collective-permute-start.5 = (f32[2,1,36,3,64]{4,2,3,1,0:T(8,128)S(1)}, f32[2,1,36,3,64]{4,2,3,1,0:T(8,128)S(1)}, u32[]{:S(2)}, u32[]{:S(2)}) collective-permute-start(f32[2,1,36,3,64]{4,2,3,1,0:T(8,128)S(1)} %pad_maximum_fusion.7), channel_id=1, source_target_pairs={{63,0},{0,1},{1,2},{2,3},{3,4},{4,5},{5,6},{6,7},{7,8},{8,9},{9,10... | collective-permute-start | bytes 165896 | tf_op jit(solution)/shard_map/ppermute | solution.py:12
  98.3 2.5 copy-start.5
  100.2 5.3 %collective-permute-start.6 = (f32[2,1,36,3,64]{4,2,3,1,0:T(8,128)S(1)}, f32[2,1,36,3,64]{4,2,3,1,0:T(8,128)S(1)}, u32[]{:S(2)}, u32[]{:S(2)}) collective-permute-start(f32[2,1,36,3,64]{4,2,3,1,0:T(8,128)S(1)} %pad_maximum_fusion.8), channel_id=1, source_target_pairs={{32,0},{33,1},{34,2},{35,3},{36,4},{37,5},{38,6},{39,7},{40,8},{41... | collective-permute-start | bytes 165896 | tf_op jit(solution)/shard_map/ppermute | solution.py:12
  100.3 10.9 %collective-permute-start.7 = (f32[2,1,36,3,64]{4,2,3,1,0:T(8,128)S(1)}, f32[2,1,36,3,64]{4,2,3,1,0:T(8,128)S(1)}, u32[]{:S(2)}, u32[]{:S(2)}) collective-permute-start(f32[2,1,36,3,64]{4,2,3,1,0:T(8,128)S(1)} %pad_maximum_fusion.8), channel_id=1, source_target_pairs={{62,0},{63,1},{0,2},{1,3},{2,4},{3,5},{4,6},{5,7},{6,8},{7,9},{8,1... | collective-permute-start | bytes 165896 | tf_op jit(solution)/shard_map/ppermute | solution.py:12
  121.5 2.9 %slice-start = ((f32[1,36,64,64]{3,1,2,0:T(8,128)}), f32[1,36,63,64]{3,1,2,0:T(8,128)S(1)}, s32[]{:S(2)}) async-start(f32[1,36,64,64]{3,1,2,0:T(8,128)} %copy-done.14), calls=%async_computation | async-start | bytes 2580480 | tf_op jit(solution)/shard_map/transpose(jvp())/split | solution.py:28
  129.6 2.9 %copy-start.8 = (f32[1,36,64,64]{3,2,0,1:T(8,128)S(1)}, f32[1,36,64,64]{3,2,0,1:T(8,128)}, u32[]{:S(2)}) copy-start(f32[1,36,64,64]{3,2,0,1:T(8,128)} %reshape.546) | copy-start | bytes 1769476
  145.3 3.0 %copy-start.18 = (f32[1,36,3,64]{2,1,3,0:T(8,128)S(1)}, f32[1,36,3,64]{2,1,3,0:T(8,128)}, u32[]{:S(2)}) copy-start(f32[1,36,3,64]{2,1,3,0:T(8,128)} %rev.88) | copy-start | bytes 82948
  154.9 10.2 %collective-permute-start.9 = (f32[2,1,36,3,64]{4,0,3,2,1:T(2,128)S(1)}, f32[2,1,36,3,64]{4,0,3,2,1:T(2,128)S(1)}, u32[]{:S(2)}, u32[]{:S(2)}) collective-permute-start(f32[2,1,36,3,64]{4,0,3,2,1:T(2,128)S(1)} %copy.228), channel_id=1, source_target_pairs={{32,0},{33,1},{34,2},{35,3},{36,4},{37,5},{38,6},{39,7},{40,8},{41... | collective-permute-start | bytes 165896 | tf_op jit(solution)/shard_map/ppermute | solution.py:12
  159.6 5.5 %collective-permute-start.8 = (f32[2,1,36,3,64]{4,0,3,2,1:T(2,128)S(1)}, f32[2,1,36,3,64]{4,0,3,2,1:T(2,128)S(1)}, u32[]{:S(2)}, u32[]{:S(2)}) collective-permute-start(f32[2,1,36,3,64]{4,0,3,2,1:T(2,128)S(1)} %copy.226), channel_id=1, source_target_pairs={{2,0},{3,1},{4,2},{5,3},{6,4},{7,5},{8,6},{9,7},{10,8},{11,9},{12,... | collective-permute-start | bytes 165896 | tf_op jit(solution)/shard_map/ppermute | solution.py:12
  187.5 4.1 %copy-start.9 = (f32[1,36,64,64]{3,2,0,1:T(8,128)S(1)}, f32[1,36,64,64]{3,2,0,1:T(8,128)}, u32[]{:S(2)}) copy-start(f32[1,36,64,64]{3,2,0,1:T(8,128)} %reshape.545) | copy-start | bytes 1769476
  187.5 4.1 %copy-start.12 = (f32[1,36,64,64]{3,1,2,0:T(8,128)S(1)}, f32[1,36,64,64]{3,1,2,0:T(8,128)}, u32[]{:S(2)}) copy-start(f32[1,36,64,64]{3,1,2,0:T(8,128)} %neg.17) | copy-start | bytes 1769476
  197.6 2.6 copy-start.15
  202.3 3.7 %copy-start.16 = (f32[1,36,3,64]{2,1,3,0:T(8,128)S(1)}, f32[1,36,3,64]{2,1,3,0:T(8,128)}, u32[]{:S(2)}) copy-start(f32[1,36,3,64]{2,1,3,0:T(8,128)} %rev.92) | copy-start | bytes 82948
  202.3 3.7 %copy-start.17 = (f32[1,36,3,64]{2,1,3,0:T(8,128)S(1)}, f32[1,36,3,64]{2,1,3,0:T(8,128)}, u32[]{:S(2)}) copy-start(f32[1,36,3,64]{2,1,3,0:T(8,128)} %rev.93) | copy-start | bytes 82948
  211.4 9.4 %collective-permute-start.10 = (f32[2,1,36,3,64]{4,0,3,2,1:T(2,128)S(1)}, f32[2,1,36,3,64]{4,0,3,2,1:T(2,128)S(1)}, u32[]{:S(2)}, u32[]{:S(2)}) collective-permute-start(f32[2,1,36,3,64]{4,0,3,2,1:T(2,128)S(1)} %copy.238), channel_id=1, source_target_pairs={{1,0},{2,1},{3,2},{4,3},{5,4},{6,5},{7,6},{8,7},{9,8},{10,9},{11,1... | collective-permute-start | bytes 165896 | tf_op jit(solution)/shard_map/ppermute | solution.py:12
  214.9 2.9 %copy-start.13 = (f32[1,36,64,64]{2,1,3,0:T(8,128)S(1)}, f32[1,36,64,64]{2,1,3,0:T(8,128)}, u32[]{:S(2)}) copy-start(f32[1,36,64,64]{2,1,3,0:T(8,128)} %copy.233) | copy-start | bytes 1769476
  217.5 5.7 %collective-permute-start.11 = (f32[2,1,36,3,64]{4,0,3,2,1:T(2,128)S(1)}, f32[2,1,36,3,64]{4,0,3,2,1:T(2,128)S(1)}, u32[]{:S(2)}, u32[]{:S(2)}) collective-permute-start(f32[2,1,36,3,64]{4,0,3,2,1:T(2,128)S(1)} %copy.239), channel_id=1, source_target_pairs={{16,0},{17,1},{18,2},{19,3},{20,4},{21,5},{22,6},{23,7},{24,8},{25... | collective-permute-start | bytes 165896 | tf_op jit(solution)/shard_map/ppermute | solution.py:12
  243.0 34.3 %copy-start.1 = (s32[6,64]{1,0:T(8,128)S(1)}, s32[6,64]{1,0:T(8,128)}, u32[]{:S(2)}) copy-start(s32[6,64]{1,0:T(8,128)} %param.25) | copy-start | bytes 4612
  (10 other events, 12.2 us)
where the time goes:
time: 283 us; the launch traced here: 278 us
  local copies, waits for them, and re-layouts  146 us (52%)
  other arithmetic  74.5 us (26%)
  waiting for transfers between devices  22.9 us (8%)
  blocking collectives  15 us (5%)
  starting transfers between devices  14.1 us (5%)
  between operations  4.68 us (2%)
    ppermute x12, waiting for transfers between devices, from_behind(): return lax.ppermute(block, axis, route)  22.9 us
    unnamed x67, local copies, waits for them, and re-layouts  20.8 us
    scatter-add x2, local copies, waits for them, and re-layouts, add_strips(): tracer_field_adjoint.at[..., side_len - 3:, :].add(north_bar[..., ::-1, :])  19.5 us
    scatter-add x2, local copies, waits for them, and re-layouts, add_strips(): tracer_field_adjoint.at[..., side_len - 3:]  17.9 us
    psum x1, blocking collectives, body(): summed_all = lax.psum(gradient, 'win')  15 us
    ppermute x6, local copies, waits for them, and re-layouts, from_behind(): return lax.ppermute(block, axis, route)  14.1 us
    ppermute x12, starting transfers between devices, from_behind(): return lax.ppermute(block, axis, route)  14.1 us
    add x2, other arithmetic, advect_along(): inflow + lax.slice_in_dim(extended, 3 - depth, 3 - depth + side_len, axis...  7.73 us
  transfers between devices with their start and end apart: 12, of which 6 were waited for; matrix products, arithmetic and copies ran while one was open for 11% of the time, Pallas kernels for 0%

commit v1 on v0

--- a/solution.py
+++ b/solution.py
@@ -169,7 +169,7 @@
             adjoint = backward_receiver_index(
                 adjoint, halo_back(rim_bar, 3), own_x, offsets_x, return_x
             )
-    summed_all = lax.psum(gradient, "win")
+    summed_all = jnp.sum(lax.all_gather(gradient, "win"), axis=0)
     row_count = gradient.shape[0] // lax.axis_size("win")
     share_rows = lax.dynamic_slice_in_dim(
         summed_all, lax.axis_index("win") * row_count, row_count, 0

time: 283 us -> 279 us (0.986)
  blocking collectives: 15 us -> 10.7 us
    psum x1 -> x0, blocking collectives: 15 us -> none  [body(): summed_all = lax.psum(gradient, 'win')]
    all_gather x0 -> x1, blocking collectives: none -> 10.7 us  [body(): summed_all = jnp.sum(lax.all_gather(gradient, 'win'), axis=0)]
where the time goes in v1:
time: 279 us; the launch traced here: 273 us
  local copies, waits for them, and re-layouts  146 us (52%)
  other arithmetic  74.6 us (27%)
  waiting for transfers between devices  22.9 us (8%)
  starting transfers between devices  14.1 us (5%)
  blocking collectives  10.7 us (4%)
  between operations  4.68 us (2%)
    ppermute x12, waiting for transfers between devices, from_behind(): return lax.ppermute(block, axis, route)  22.9 us
    unnamed x67, local copies, waits for them, and re-layouts  20.8 us
    scatter-add x2, local copies, waits for them, and re-layouts, add_strips(): tracer_field_adjoint.at[..., side_len - 3:, :].add(north_bar[..., ::-1, :])  19.5 us
    scatter-add x2, local copies, waits for them, and re-layouts, add_strips(): tracer_field_adjoint.at[..., side_len - 3:]  17.9 us
    ppermute x6, local copies, waits for them, and re-layouts, from_behind(): return lax.ppermute(block, axis, route)  14.1 us
    ppermute x12, starting transfers between devices, from_behind(): return lax.ppermute(block, axis, route)  14.1 us
    all_gather x1, blocking collectives, body(): summed_all = jnp.sum(lax.all_gather(gradient, 'win'), axis=0)  10.7 us
    add x2, other arithmetic, advect_along(): inflow + lax.slice_in_dim(extended, 3 - depth, 3 - depth + side_len, axis...  7.73 us
  transfers between devices with their start and end apart: 12, of which 6 were waited for; matrix products, arithmetic and copies ran while one was open for 11% of the time, Pallas kernels for 0%

profile of v1, /device:TPU:1, one launch (start us, length us, event | category | flops | bytes accessed | tf_op | source)
XLA Modules:
  0.0 273.3 jit_solution(8202946030276359137)
XLA Ops:
  27.1 3.3 %rev.75 = f32[1,36,3,64]{2,1,3,0:T(8,128)} reverse(f32[1,36,3,64]{2,1,3,0:T(8,128)} %reverse_select_fusion.1), dimensions={2} | reverse | bytes 55296 | tf_op jit(solution)/shard_map/rev | solution.py:62
  30.5 5.5 %fusion.53 = (f32[1,36,64,64]{3,1,2,0:T(8,128)S(1)}, f32[1,36,64,64]{3,1,2,0:T(8,128)}) fusion(f32[1,36,64,64]{3,2,0,1:T(8,128)} %reshape.557, f32[1,36,64,64]{3,1,2,0:T(8,128)S(1)} %copy.222, f32[1,36,64,3]{3,1,2,0:T(8,128)} %bitcast.82), kind=kLoop, calls=%fused_computation.160 | loop fusion | flops 1916928 | bytes 2386944 | tf_op jit(solution)/shard_map/convert_element_type | solution.py:120
  40.8 2.8 %fusion.24 = f32[1,36,64,1]{3,1,2,0:T(8,128)S(1)} fusion(f32[1,36,64,1]{3,1,2,0:T(8,128)} %copy.221, f32[1,36,64,64]{3,1,2,0:T(8,128)S(1)} %copy.222, f32[1,36,64,64]{3,1,2,0:T(8,128)S(1)} %get-tuple-element.82), kind=kLoop, calls=%fused_computation.53 | loop fusion | flops 18432 | bytes 55296 | tf_op jit(solution)/shard_map/add | solution.py:25
  56.4 7.5 %collective-permute-done.3 = f32[2,1,36,3,64]{4,2,3,1,0:T(8,128)S(1)} collective-permute-done((f32[2,1,36,3,64]{4,2,3,1,0:T(8,128)S(1)}, f32[2,1,36,3,64]{4,2,3,1,0:T(8,128)S(1)}, u32[]{:S(2)}, u32[]{:S(2)}) %collective-permute-start.3) | collective-permute-done | bytes 55328 | tf_op jit(solution)/shard_map/ppermute | solution.py:12
  72.0 3.8 %fusion.17 = f32[1,36,64,1]{3,1,2,0:T(8,128)} fusion(f32[1,36,64,1]{3,1,2,0:T(8,128)} %copy.221, f32[1,36,64,64]{3,1,2,0:T(8,128)S(1)} %multiply_add_fusion.1, f32[1,36,64,64]{3,1,2,0:T(8,128)S(1)} %get-tuple-element.82), kind=kLoop, calls=%fused_computation.38 | loop fusion | flops 18432 | bytes 55296 | tf_op jit(solution)/shard_map/add | solution.py:25
  87.2 3.3 %rev.83 = f32[1,36,3,64]{2,1,3,0:T(8,128)} reverse(f32[1,36,3,64]{2,1,3,0:T(8,128)} %reverse_select_fusion), dimensions={2} | reverse | bytes 55296 | tf_op jit(solution)/shard_map/rev | solution.py:62
  90.5 4.4 %fusion.20 = f32[1,36,64,64]{3,1,2,0:T(8,128)S(1)} fusion(f32[1,36,64,64]{3,1,2,0:T(8,128)S(1)} %multiply_add_fusion.1, f32[1,36,64,3]{3,1,2,0:T(8,128)} %bitcast.81, f32[1,36,64,64]{3,2,0,1:T(8,128)} %reshape.557), kind=kLoop, calls=%fused_computation.44 | loop fusion | flops 1916928 | bytes 1797120 | tf_op jit(solution)/shard_map/add | solution.py:22
  101.5 4.0 %collective-permute-done.6 = f32[2,1,36,3,64]{4,2,3,1,0:T(8,128)S(1)} collective-permute-done((f32[2,1,36,3,64]{4,2,3,1,0:T(8,128)S(1)}, f32[2,1,36,3,64]{4,2,3,1,0:T(8,128)S(1)}, u32[]{:S(2)}, u32[]{:S(2)}) %collective-permute-start.6) | collective-permute-done | bytes 55328 | tf_op jit(solution)/shard_map/ppermute | solution.py:12
  105.5 5.7 %collective-permute-done.7 = f32[2,1,36,3,64]{4,2,3,1,0:T(8,128)S(1)} collective-permute-done((f32[2,1,36,3,64]{4,2,3,1,0:T(8,128)S(1)}, f32[2,1,36,3,64]{4,2,3,1,0:T(8,128)S(1)}, u32[]{:S(2)}, u32[]{:S(2)}) %collective-permute-start.7) | collective-permute-done | bytes 55328 | tf_op jit(solution)/shard_map/ppermute | solution.py:12
  111.4 3.3 %fusion.5 = (f32[1,36,64,64]{3,1,2,0:T(8,128)S(1)}, f32[1,36,64,64]{3,1,2,0:T(8,128)}) fusion(f32[1,36,64,64]{3,1,2,0:T(8,128)S(1)} %copy-done.5, f32[1,36,3,64]{3,1,2,0:T(8,128)S(1)} %rev.87, f32[1,36,64,64]{3,2,0,1:T(8,128)} %reshape.558), kind=kLoop, calls=%fused_computation.20 | loop fusion | flops 1916928 | bytes 2386944 | tf_op jit(solution)/shard_map/add | solution.py:22
  121.5 2.9 %copy.241 = f32[1,36,64,64]{2,1,3,0:T(8,128)} copy(f32[1,36,64,64]{3,1,2,0:T(8,128)} %get-tuple-element.79) | data formatting | bytes 1179648 | tf_op jit(solution)/shard_map/jit(clip)/min | solution.py:24
  126.0 3.6 %fusion.51 = (f32[1,36,64,64]{2,1,3,0:T(8,128)}, f32[1,36,64,64]{2,1,3,0:T(8,128)}) fusion(f32[1,36,64,64]{2,1,3,0:T(8,128)} %copy.241, f32[1,36,63,64]{2,1,3,0:T(8,128)} %copy.298, f32[36]{0:T(128)S(1)} %broadcast_divide_fusion, f32[64,64]{0,1:T(8,128)S(1)} %copy.234), kind=kLoop, calls=%fused_computation.158 | loop fusion | flops 442368 | bytes 2366608 | tf_op jit(solution)/shard_map/transpose(jvp())/mul | solution.py:22
  129.6 2.9 %copy.239 = f32[1,36,64,64]{3,1,2,0:T(8,128)} copy(f32[1,36,64,64]{2,1,3,0:T(8,128)} %get-tuple-element.56) | data formatting | bytes 1179648 | tf_op jit(solution)/shard_map/transpose(jvp())/add_any | solution.py:28
  140.1 2.6 rev.88
  142.7 2.6 rev.89
  145.3 2.9 %copy.275 = f32[1,36,64,64]{3,1,2,0:T(8,128)} copy(f32[1,36,64,64]{2,1,3,0:T(8,128)} %split.34) | data formatting | bytes 1179648
  149.7 2.7 pad_maximum_fusion
  156.9 2.6 copy.247
  166.7 17.9 %scatter-add.14 = f32[1,36,64,64]{3,1,2,0:T(8,128)S(1)} dynamic-update-slice(f32[1,36,64,64]{3,1,2,0:T(8,128)S(1)} %add_add_fusion, f32[1,36,64,3]{3,1,2,0:T(8,128)} %copy.253, s32[]{:T(128)} %constant.141.clone.1, s32[]{:T(128)} %constant.141.clone.1, s32[]{:T(128)} %constant.141.clone.1, s32[]{:T(128)} %constant.153.clone.1) | dynamic-update-slice | bytes 55300 | tf_op jit(solution)/shard_map/scatter-add | solution.py:54
  187.5 4.1 %fusion.40 = (f32[1,36,64,1]{3,1,2,0:T(8,128)}, f32[1,36,64,1]{3,1,2,0:T(8,128)}, f32[1,36,64,1]{3,1,2,0:T(8,128)}) fusion(f32[1,36,64,64]{3,1,2,0:T(8,128)S(1)} %get-tuple-element.82, f32[1,36,64,64]{3,1,2,0:T(8,128)} %neg.17), kind=kLoop, calls=%fused_computation.103 | loop fusion | flops 11520 | bytes 46080 | tf_op jit(solution)/shard_map/transpose(jvp())/mul | solution.py:25
  195.0 2.6 rev.92
  197.6 2.6 rev.93
  206.2 2.7 fusion
  211.4 3.5 %collective-permute-start.10 = (f32[2,1,36,3,64]{4,0,3,2,1:T(2,128)S(1)}, f32[2,1,36,3,64]{4,0,3,2,1:T(2,128)S(1)}, u32[]{:S(2)}, u32[]{:S(2)}) collective-permute-start(f32[2,1,36,3,64]{4,0,3,2,1:T(2,128)S(1)} %copy.260), channel_id=1, source_target_pairs={{1,0},{2,1},{3,2},{4,3},{5,4},{6,5},{7,6},{8,7},{9,8},{10,9},{11,1... | collective-permute-start | bytes 165896 | tf_op jit(solution)/shard_map/ppermute | solution.py:12
  214.9 2.6 copy.261
  225.5 2.8 %add.209 = f32[2,1,36,3,64]{3,2,4,1,0:T(8,128)S(1)} add(f32[2,1,36,3,64]{3,2,4,1,0:T(8,128)} %copy.262, f32[2,1,36,3,64]{3,2,4,1,0:T(8,128)} %copy.263) | non-fusion elementwise | flops 13824 | bytes 165888 | tf_op jit(solution)/shard_map/add | solution.py:112
  229.6 3.3 %rev.94 = f32[1,36,64,3]{3,1,2,0:T(8,128)} reverse(f32[1,36,64,3]{3,1,2,0:T(8,128)} %get-tuple-element.61), dimensions={3} | reverse | bytes 55296 | tf_op jit(solution)/shard_map/rev | solution.py:55
  232.9 2.9 %add.210 = f32[1,36,64,3]{3,1,2,0:T(8,128)} add(f32[1,36,64,3]{3,1,2,0:T(8,128)} %copy.277, f32[1,36,64,3]{3,1,2,0:T(8,128)} %rev.94) | non-fusion elementwise | flops 6912 | bytes 82944 | tf_op jit(solution)/shard_map/add | solution.py:54
  237.6 2.6 rev.95
  240.2 2.8 %slice_add_fusion = f32[1,36,3,64]{2,1,3,0:T(8,128)} fusion(f32[1,36,3,64]{2,1,3,0:T(8,128)} %rev.95, f32[1,36,64,64]{2,1,3,0:T(8,128)S(1)} %constant_dynamic-update-slice_fusion), kind=kLoop, calls=%fused_computation.32 | loop fusion | flops 6912 | bytes 82944 | tf_op jit(solution)/shard_map/add | solution.py:57
  243.0 18.0 %scatter-add.19 = f32[1,36,64,64]{2,1,3,0:T(8,128)S(1)} dynamic-update-slice(f32[1,36,64,64]{2,1,3,0:T(8,128)S(1)} %constant_dynamic-update-slice_fusion, f32[1,36,3,64]{2,1,3,0:T(8,128)} %slice_add_fusion, s32[]{:T(128)} %constant.141.clone.1, s32[]{:T(128)} %constant.141.clone.1, s32[]{:T(128)} %constant.153.clone.1, s32[]{:T(128)} %constant.141.clone.1) | dynamic-update-slice | bytes 55300 | tf_op jit(solution)/shard_map/scatter-add | solution.py:57
  261.7 10.7 %all-gather = f32[256,64]{1,0:T(8,128)S(1)} all-gather(f32[64,64]{1,0:T(8,128)S(1)} %copy.266), channel_id=2, replica_groups=mesh['win'=4,'tile'=64] {'win'}, dimensions={0}, use_global_device_ids=true | all-gather | bytes 81920 | tf_op jit(solution)/shard_map/all_gather | solution.py:172
  (199 shorter events, 122.9 us)
Async XLA Ops:
  0.0 11.2 %copy-start = (s32[6,64]{1,0:T(8,128)S(1)}, s32[6,64]{1,0:T(8,128)}, u32[]{:S(2)}) copy-start(s32[6,64]{1,0:T(8,128)} %param.25) | copy-start | bytes 4612
  3.0 8.9 %copy-start.6 = (f32[1,36,64,64]{3,2,0,1:T(8,128)}, f32[1,36,64,64]{3,2,0,1:T(8,128)S(1)}, u32[]{:S(2)}) copy-start(f32[1,36,64,64]{3,2,0,1:T(8,128)S(1)} %reshape_squeeze.3) | copy-start | bytes 1769476
  7.3 5.3 %copy-start.22 = (bf16[1,1,36,4096]{3,2,1,0:T(8,128)(2,1)S(1)}, bf16[1,1,36,4096]{3,2,1,0:T(8,128)(2,1)}, u32[]{:S(2)}) copy-start(bf16[1,1,36,4096]{3,2,1,0:T(8,128)(2,1)} %param.18) | copy-start | bytes 884740
  7.3 9.4 %collective-permute-start = (f32[2,1,36,3,64]{4,0,3,2,1:T(2,128)S(1)}, f32[2,1,36,3,64]{4,0,3,2,1:T(2,128)S(1)}, u32[]{:S(2)}, u32[]{:S(2)}) collective-permute-start(f32[2,1,36,3,64]{4,0,3,2,1:T(2,128)S(1)} %pad_maximum_fusion.9), channel_id=1, source_target_pairs={{48,0},{49,1},{50,2},{51,3},{52,4},{53,5},{54,6},{55,7},{56,8},{57... | collective-permute-start | bytes 165896 | tf_op jit(solution)/shard_map/ppermute | solution.py:12
  9.4 12.0 %collective-permute-start.1 = (f32[2,1,36,3,64]{4,0,3,2,1:T(2,128)S(1)}, f32[2,1,36,3,64]{4,0,3,2,1:T(2,128)S(1)}, u32[]{:S(2)}, u32[]{:S(2)}) collective-permute-start(f32[2,1,36,3,64]{4,0,3,2,1:T(2,128)S(1)} %pad_maximum_fusion.9), channel_id=1, source_target_pairs={{63,0},{0,1},{1,2},{2,3},{3,4},{4,5},{5,6},{6,7},{7,8},{8,9},{9,10... | collective-permute-start | bytes 165896 | tf_op jit(solution)/shard_map/ppermute | solution.py:12
  12.6 3.5 %copy-start.28 = (f32[36]{0:T(128)S(1)}, f32[36]{0:T(128)}, u32[]{:S(2)}) copy-start(f32[36]{0:T(128)} %param.22) | copy-start | bytes 436
  40.7 2.8 %copy-start.11 = (f32[1,36,64,64]{3,1,2,0:T(8,128)S(1)}, f32[1,36,64,64]{3,1,2,0:T(8,128)}, u32[]{:S(2)}) copy-start(f32[1,36,64,64]{3,1,2,0:T(8,128)} %get-tuple-element.83) | copy-start | bytes 1769476
  45.8 20.6 %copy-start.2 = (f32[1,36,64,64]{3,1,2,0:T(8,128)}, f32[1,36,64,64]{3,1,2,0:T(8,128)S(1)}, u32[]{:S(2)}) copy-start(f32[1,36,64,64]{3,1,2,0:T(8,128)S(1)} %fusion.30) | copy-start | bytes 1769476
  47.3 5.9 %copy-start.23 = (bf16[1,1,36,4096]{3,2,1,0:T(8,128)(2,1)S(1)}, bf16[1,1,36,4096]{3,2,1,0:T(8,128)(2,1)}, u32[]{:S(2)}) copy-start(bf16[1,1,36,4096]{3,2,1,0:T(8,128)(2,1)} %param.19) | copy-start | bytes 884740
  49.1 7.3 %collective-permute-start.2 = (f32[2,1,36,3,64]{4,2,3,1,0:T(8,128)S(1)}, f32[2,1,36,3,64]{4,2,3,1,0:T(8,128)S(1)}, u32[]{:S(2)}, u32[]{:S(2)}) collective-permute-start(f32[2,1,36,3,64]{4,2,3,1,0:T(8,128)S(1)} %pad_maximum_fusion.6), channel_id=1, source_target_pairs={{32,0},{33,1},{34,2},{35,3},{36,4},{37,5},{38,6},{39,7},{40,8},{41... | collective-permute-start | bytes 165896 | tf_op jit(solution)/shard_map/ppermute | solution.py:12
  50.7 13.2 %collective-permute-start.3 = (f32[2,1,36,3,64]{4,2,3,1,0:T(8,128)S(1)}, f32[2,1,36,3,64]{4,2,3,1,0:T(8,128)S(1)}, u32[]{:S(2)}, u32[]{:S(2)}) collective-permute-start(f32[2,1,36,3,64]{4,2,3,1,0:T(8,128)S(1)} %pad_maximum_fusion.6), channel_id=1, source_target_pairs={{62,0},{63,1},{0,2},{1,3},{2,4},{3,5},{4,6},{5,7},{6,8},{7,9},{8,1... | collective-permute-start | bytes 165896 | tf_op jit(solution)/shard_map/ppermute | solution.py:12
  66.4 1.8 copy-start.3
  66.4 1.8 copy-start.24
  71.8 5.0 %collective-permute-start.4 = (f32[2,1,36,3,64]{4,2,3,1,0:T(8,128)S(1)}, f32[2,1,36,3,64]{4,2,3,1,0:T(8,128)S(1)}, u32[]{:S(2)}, u32[]{:S(2)}) collective-permute-start(f32[2,1,36,3,64]{4,2,3,1,0:T(8,128)S(1)} %pad_maximum_fusion.7), channel_id=1, source_target_pairs={{48,0},{49,1},{50,2},{51,3},{52,4},{53,5},{54,6},{55,7},{56,8},{57... | collective-permute-start | bytes 165896 | tf_op jit(solution)/shard_map/ppermute | solution.py:12
  71.9 9.5 %collective-permute-start.5 = (f32[2,1,36,3,64]{4,2,3,1,0:T(8,128)S(1)}, f32[2,1,36,3,64]{4,2,3,1,0:T(8,128)S(1)}, u32[]{:S(2)}, u32[]{:S(2)}) collective-permute-start(f32[2,1,36,3,64]{4,2,3,1,0:T(8,128)S(1)} %pad_maximum_fusion.7), channel_id=1, source_target_pairs={{63,0},{0,1},{1,2},{2,3},{3,4},{4,5},{5,6},{6,7},{7,8},{8,9},{9,10... | collective-permute-start | bytes 165896 | tf_op jit(solution)/shard_map/ppermute | solution.py:12
  98.3 2.5 copy-start.5
  100.2 5.3 %collective-permute-start.6 = (f32[2,1,36,3,64]{4,2,3,1,0:T(8,128)S(1)}, f32[2,1,36,3,64]{4,2,3,1,0:T(8,128)S(1)}, u32[]{:S(2)}, u32[]{:S(2)}) collective-permute-start(f32[2,1,36,3,64]{4,2,3,1,0:T(8,128)S(1)} %pad_maximum_fusion.8), channel_id=1, source_target_pairs={{32,0},{33,1},{34,2},{35,3},{36,4},{37,5},{38,6},{39,7},{40,8},{41... | collective-permute-start | bytes 165896 | tf_op jit(solution)/shard_map/ppermute | solution.py:12
  100.3 10.9 %collective-permute-start.7 = (f32[2,1,36,3,64]{4,2,3,1,0:T(8,128)S(1)}, f32[2,1,36,3,64]{4,2,3,1,0:T(8,128)S(1)}, u32[]{:S(2)}, u32[]{:S(2)}) collective-permute-start(f32[2,1,36,3,64]{4,2,3,1,0:T(8,128)S(1)} %pad_maximum_fusion.8), channel_id=1, source_target_pairs={{62,0},{63,1},{0,2},{1,3},{2,4},{3,5},{4,6},{5,7},{6,8},{7,9},{8,1... | collective-permute-start | bytes 165896 | tf_op jit(solution)/shard_map/ppermute | solution.py:12
  121.5 2.9 %slice-start = ((f32[1,36,64,64]{3,1,2,0:T(8,128)}), f32[1,36,63,64]{3,1,2,0:T(8,128)S(1)}, s32[]{:S(2)}) async-start(f32[1,36,64,64]{3,1,2,0:T(8,128)} %copy-done.14), calls=%async_computation | async-start | bytes 2580480 | tf_op jit(solution)/shard_map/transpose(jvp())/split | solution.py:28
  129.6 2.9 %copy-start.8 = (f32[1,36,64,64]{3,2,0,1:T(8,128)S(1)}, f32[1,36,64,64]{3,2,0,1:T(8,128)}, u32[]{:S(2)}) copy-start(f32[1,36,64,64]{3,2,0,1:T(8,128)} %reshape.558) | copy-start | bytes 1769476
  145.3 3.0 %copy-start.18 = (f32[1,36,3,64]{2,1,3,0:T(8,128)S(1)}, f32[1,36,3,64]{2,1,3,0:T(8,128)}, u32[]{:S(2)}) copy-start(f32[1,36,3,64]{2,1,3,0:T(8,128)} %rev.88) | copy-start | bytes 82948
  154.9 10.2 %collective-permute-start.9 = (f32[2,1,36,3,64]{4,0,3,2,1:T(2,128)S(1)}, f32[2,1,36,3,64]{4,0,3,2,1:T(2,128)S(1)}, u32[]{:S(2)}, u32[]{:S(2)}) collective-permute-start(f32[2,1,36,3,64]{4,0,3,2,1:T(2,128)S(1)} %copy.250), channel_id=1, source_target_pairs={{32,0},{33,1},{34,2},{35,3},{36,4},{37,5},{38,6},{39,7},{40,8},{41... | collective-permute-start | bytes 165896 | tf_op jit(solution)/shard_map/ppermute | solution.py:12
  159.6 5.5 %collective-permute-start.8 = (f32[2,1,36,3,64]{4,0,3,2,1:T(2,128)S(1)}, f32[2,1,36,3,64]{4,0,3,2,1:T(2,128)S(1)}, u32[]{:S(2)}, u32[]{:S(2)}) collective-permute-start(f32[2,1,36,3,64]{4,0,3,2,1:T(2,128)S(1)} %copy.248), channel_id=1, source_target_pairs={{2,0},{3,1},{4,2},{5,3},{6,4},{7,5},{8,6},{9,7},{10,8},{11,9},{12,... | collective-permute-start | bytes 165896 | tf_op jit(solution)/shard_map/ppermute | solution.py:12
  187.5 4.1 %copy-start.9 = (f32[1,36,64,64]{3,2,0,1:T(8,128)S(1)}, f32[1,36,64,64]{3,2,0,1:T(8,128)}, u32[]{:S(2)}) copy-start(f32[1,36,64,64]{3,2,0,1:T(8,128)} %reshape.557) | copy-start | bytes 1769476
  187.5 4.1 %copy-start.12 = (f32[1,36,64,64]{3,1,2,0:T(8,128)S(1)}, f32[1,36,64,64]{3,1,2,0:T(8,128)}, u32[]{:S(2)}) copy-start(f32[1,36,64,64]{3,1,2,0:T(8,128)} %neg.17) | copy-start | bytes 1769476
  197.6 2.6 copy-start.15
  202.3 3.7 %copy-start.16 = (f32[1,36,3,64]{2,1,3,0:T(8,128)S(1)}, f32[1,36,3,64]{2,1,3,0:T(8,128)}, u32[]{:S(2)}) copy-start(f32[1,36,3,64]{2,1,3,0:T(8,128)} %rev.92) | copy-start | bytes 82948
  202.3 3.7 %copy-start.17 = (f32[1,36,3,64]{2,1,3,0:T(8,128)S(1)}, f32[1,36,3,64]{2,1,3,0:T(8,128)}, u32[]{:S(2)}) copy-start(f32[1,36,3,64]{2,1,3,0:T(8,128)} %rev.93) | copy-start | bytes 82948
  211.4 9.4 %collective-permute-start.10 = (f32[2,1,36,3,64]{4,0,3,2,1:T(2,128)S(1)}, f32[2,1,36,3,64]{4,0,3,2,1:T(2,128)S(1)}, u32[]{:S(2)}, u32[]{:S(2)}) collective-permute-start(f32[2,1,36,3,64]{4,0,3,2,1:T(2,128)S(1)} %copy.260), channel_id=1, source_target_pairs={{1,0},{2,1},{3,2},{4,3},{5,4},{6,5},{7,6},{8,7},{9,8},{10,9},{11,1... | collective-permute-start | bytes 165896 | tf_op jit(solution)/shard_map/ppermute | solution.py:12
  214.9 2.9 %copy-start.13 = (f32[1,36,64,64]{2,1,3,0:T(8,128)S(1)}, f32[1,36,64,64]{2,1,3,0:T(8,128)}, u32[]{:S(2)}) copy-start(f32[1,36,64,64]{2,1,3,0:T(8,128)} %copy.255) | copy-start | bytes 1769476
  217.5 5.7 %collective-permute-start.11 = (f32[2,1,36,3,64]{4,0,3,2,1:T(2,128)S(1)}, f32[2,1,36,3,64]{4,0,3,2,1:T(2,128)S(1)}, u32[]{:S(2)}, u32[]{:S(2)}) collective-permute-start(f32[2,1,36,3,64]{4,0,3,2,1:T(2,128)S(1)} %copy.261), channel_id=1, source_target_pairs={{16,0},{17,1},{18,2},{19,3},{20,4},{21,5},{22,6},{23,7},{24,8},{25... | collective-permute-start | bytes 165896 | tf_op jit(solution)/shard_map/ppermute | solution.py:12
  243.0 30.0 %copy-start.1 = (s32[6,64]{1,0:T(8,128)S(1)}, s32[6,64]{1,0:T(8,128)}, u32[]{:S(2)}) copy-start(s32[6,64]{1,0:T(8,128)} %param.25) | copy-start | bytes 4612
  (10 other events, 12.2 us)
